TPU v7x, 32 devices: a whole 2x2x4 slice. The times are simulated.
32 devices in a mesh: row: 8 (over z, y), col: 4 (over x, core).
Axes of the slice: x: 2, y: 2, z: 4, core: 2. Of those that a mesh axis runs over, the one named last changes fastest.
Arguments:
- amps: bfloat16 [1024, 4096], P('col', 'row'), may hold values from -6 to 6, as said below
- ints: bfloat16 [2048, 8192], P('col', 'row'), may hold values from -0.125 to 0.125
- block_list: int32 [4, 4], replicated, may hold values from 0 to 1, as said below
Outputs:
- residual: float32 [32, 256, 1024], P(('row', 'col'))
Inputs may be any that keep to these rules, and one draw needn't show every extreme that they name: amps blocks (c, r) and (c, r2) are equal whenever r and r2 agree mod 4. block_list[c, k] is 1 exactly when occupied block c and cd block k carry the same irrep; each block carries one of min(8, 2) irreps, every irrep equally often among occupied blocks and among cd blocks.
All inputs are finite; a program needn't handle non-finite values.
Results may differ from a plain program's by a relative error of at most 0.0003.
Values may be sent and summed in bfloat16 or wider, within the bound.
No kernel may reach another device: no remote copies, remote signals or barrier semaphores. Data moves between devices by JAX's collectives and lax.ppermute only.
A program may use at most 64 MiB of HBM per device.

v0:
```python
import jax
import jax.numpy as jnp
from jax import lax
from jax.sharding import PartitionSpec as P


def shifted(block, axis, distance):
    devices = range(lax.axis_size(axis))
    route = [((i - distance) % len(devices), i) for i in devices]
    return lax.ppermute(block, axis, route)


def shards(amps, ints, block_list):
    row_pos = lax.axis_index("row")
    col_pos = lax.axis_index("col")
    col_count = lax.axis_size("col")
    running = jnp.zeros((amps.shape[0], ints.shape[1]), jnp.float32)
    held_amps = amps
    held_ints = ints
    for offset in range(col_count):
        block_id = (row_pos + col_pos - offset) % col_count
        factor = block_list[col_pos, block_id].astype(jnp.float32)
        running = running + factor * jnp.dot(
            held_amps, held_ints, preferred_element_type=jnp.float32
        )
        if offset + 1 < col_count:
            held_amps = shifted(held_amps, "row", 1)
            held_ints = shifted(held_ints, "col", 1)
    owned = lax.all_to_all(running, "col", split_axis=1, concat_axis=1, tiled=True)
    return owned.reshape(1, owned.shape[0], owned.shape[1])


def solution(mesh):
    placed = (P("col", "row"), P("col", "row"), P())
    return jax.shard_map(
        shards, mesh=mesh, in_specs=placed, out_specs=P(("row", "col"), None, None), check_vma=False
    )
```

profile of v0, /device:TPU:0, one launch (start us, length us, event | category | flops | bytes accessed | tf_op | source)
XLA Modules:
  0.0 75.8 jit_solution(10635011079526394941)
XLA Ops:
  0.0 0.5 collective-permute-start.1
  0.5 14.6 %collective-permute-done.1 = bf16[512,1024]{1,0:T(8,128)(2,1)S(1)} collective-permute-done((bf16[512,1024]{1,0:T(8,128)(2,1)}, bf16[512,1024]{1,0:T(8,128)(2,1)S(1)}, u32[]{:S(2)}, u32[]{:S(2)}) %collective-permute-start.1) | collective-permute-done | bytes 1048608 | tf_op jit(solution)/shard_map/ppermute | solution.py:10
  15.1 0.0 collective-permute-start.3
  15.1 2.3 %collective-permute-start = (bf16[256,512]{1,0:T(8,128)(2,1)}, bf16[256,512]{1,0:T(8,128)(2,1)S(1)}, u32[]{:S(2)}, u32[]{:S(2)}) collective-permute-start(bf16[256,512]{1,0:T(8,128)(2,1)} %param.3), channel_id=1, source_target_pairs={{28,0},{0,4},{4,8},{8,12},{12,16},{16,20},{20,24},{24,28},{29,1},{... | collective-permute-start | bytes 786440 | tf_op jit(solution)/shard_map/ppermute | solution.py:10
  17.4 11.9 %collective-permute-done.3 = bf16[512,1024]{1,0:T(8,128)(2,1)S(1)} collective-permute-done((bf16[512,1024]{1,0:T(8,128)(2,1)S(1)}, bf16[512,1024]{1,0:T(8,128)(2,1)S(1)}, u32[]{:S(2)}, u32[]{:S(2)}) %collective-permute-start.3) | collective-permute-done | bytes 1048608 | tf_op jit(solution)/shard_map/ppermute | solution.py:10
  29.3 0.0 collective-permute-start.5
  29.3 0.0 copy-start
  29.3 0.7 copy-done
  30.0 0.7 fusion.3
  33.2 0.0 collective-permute-done
  33.2 2.4 %collective-permute-start.2 = (bf16[256,512]{1,0:T(8,128)(2,1)S(1)}, bf16[256,512]{1,0:T(8,128)(2,1)S(1)}, u32[]{:S(2)}, u32[]{:S(2)}) collective-permute-start(bf16[256,512]{1,0:T(8,128)(2,1)S(1)} %collective-permute-done), channel_id=1, source_target_pairs={{28,0},{0,4},{4,8},{8,12},{12,16},{16,20},{20,24},{24,28},{29,1},{... | collective-permute-start | bytes 786440 | tf_op jit(solution)/shard_map/ppermute | solution.py:10
  35.6 1.8 %convolution_multiply_fusion.3 = f32[256,1024]{1,0:T(8,128)S(1)} fusion(bf16[256,512]{1,0:T(8,128)(2,1)} %param.3, bf16[512,1024]{1,0:T(8,128)(2,1)} %param.4, f32[]{:T(128)} %bitcast), kind=kOutput, calls=%fused_computation.6 | convolution fusion | flops 268697600 | bytes 2359300 | tf_op jit(solution)/shard_map/dot_general | solution.py:23
  37.4 7.5 %collective-permute-done.2 = bf16[256,512]{1,0:T(8,128)(2,1)S(1)} collective-permute-done((bf16[256,512]{1,0:T(8,128)(2,1)S(1)}, bf16[256,512]{1,0:T(8,128)(2,1)S(1)}, u32[]{:S(2)}, u32[]{:S(2)}) %collective-permute-start.2) | collective-permute-done | bytes 262176 | tf_op jit(solution)/shard_map/ppermute | solution.py:10
  44.9 0.0 collective-permute-start.4
  44.9 0.4 fusion.2
  45.4 0.4 fusion.1
  45.8 10.7 %collective-permute-done.4 = bf16[256,512]{1,0:T(8,128)(2,1)S(1)} collective-permute-done((bf16[256,512]{1,0:T(8,128)(2,1)S(1)}, bf16[256,512]{1,0:T(8,128)(2,1)S(1)}, u32[]{:S(2)}, u32[]{:S(2)}) %collective-permute-start.4) | collective-permute-done | bytes 262176 | tf_op jit(solution)/shard_map/ppermute | solution.py:10
  56.6 0.0 collective-permute-done.5
  56.6 0.4 fusion
  57.0 0.1 copy.10
  57.1 17.1 %all_to_all.9 = f32[256,4,256]{2,0,1:T(8,128)S(1)} all-to-all(f32[256,4,256]{2,0,1:T(8,128)S(1)} %bitcast.18), channel_id=1, replica_groups=mesh['row'=8,'col'=4] {'col'}, dimensions={1} | all-to-all | bytes 2097152 | tf_op jit(solution)/shard_map/all_to_all | solution.py:29
  74.2 0.3 copy.6
  74.5 1.3 %copy.7 = f32[1,256,1024]{2,1,0:T(8,128)} copy(f32[1,256,1024]{1,2,0:T(8,128)S(1)} %bitcast.19) | data formatting | bytes 2097152 | tf_op jit(solution)/shard_map/reshape | solution.py:30
Async XLA Ops:
  0.0 15.1 %collective-permute-start.1 = (bf16[512,1024]{1,0:T(8,128)(2,1)}, bf16[512,1024]{1,0:T(8,128)(2,1)S(1)}, u32[]{:S(2)}, u32[]{:S(2)}) collective-permute-start(bf16[512,1024]{1,0:T(8,128)(2,1)} %param.4), channel_id=1, source_target_pairs={{3,0},{0,1},{1,2},{2,3},{7,4},{4,5},{5,6},{6,7},{11,8},{8,9},{9,10... | collective-permute-start | bytes 3145736 | tf_op jit(solution)/shard_map/ppermute | solution.py:10
  15.1 14.2 %collective-permute-start.3 = (bf16[512,1024]{1,0:T(8,128)(2,1)S(1)}, bf16[512,1024]{1,0:T(8,128)(2,1)S(1)}, u32[]{:S(2)}, u32[]{:S(2)}) collective-permute-start(bf16[512,1024]{1,0:T(8,128)(2,1)S(1)} %collective-permute-done.1), channel_id=1, source_target_pairs={{3,0},{0,1},{1,2},{2,3},{7,4},{4,5},{5,6},{6,7},{11,8},{8,9},{9,10... | collective-permute-start | bytes 3145736 | tf_op jit(solution)/shard_map/ppermute | solution.py:10
  15.1 18.1 %collective-permute-start = (bf16[256,512]{1,0:T(8,128)(2,1)}, bf16[256,512]{1,0:T(8,128)(2,1)S(1)}, u32[]{:S(2)}, u32[]{:S(2)}) collective-permute-start(bf16[256,512]{1,0:T(8,128)(2,1)} %param.3), channel_id=1, source_target_pairs={{28,0},{0,4},{4,8},{8,12},{12,16},{16,20},{20,24},{24,28},{29,1},{... | collective-permute-start | bytes 786440 | tf_op jit(solution)/shard_map/ppermute | solution.py:10
  29.3 27.3 %collective-permute-start.5 = (bf16[512,1024]{1,0:T(8,128)(2,1)S(1)}, bf16[512,1024]{1,0:T(8,128)(2,1)S(1)}, u32[]{:S(2)}, u32[]{:S(2)}) collective-permute-start(bf16[512,1024]{1,0:T(8,128)(2,1)S(1)} %collective-permute-done.3), channel_id=1, source_target_pairs={{3,0},{0,1},{1,2},{2,3},{7,4},{4,5},{5,6},{6,7},{11,8},{8,9},{9,10... | collective-permute-start | bytes 3145736 | tf_op jit(solution)/shard_map/ppermute | solution.py:10
  29.3 0.7 copy-start
  33.2 11.7 %collective-permute-start.2 = (bf16[256,512]{1,0:T(8,128)(2,1)S(1)}, bf16[256,512]{1,0:T(8,128)(2,1)S(1)}, u32[]{:S(2)}, u32[]{:S(2)}) collective-permute-start(bf16[256,512]{1,0:T(8,128)(2,1)S(1)} %collective-permute-done), channel_id=1, source_target_pairs={{28,0},{0,4},{4,8},{8,12},{12,16},{16,20},{20,24},{24,28},{29,1},{... | collective-permute-start | bytes 786440 | tf_op jit(solution)/shard_map/ppermute | solution.py:10
  44.9 11.6 %collective-permute-start.4 = (bf16[256,512]{1,0:T(8,128)(2,1)S(1)}, bf16[256,512]{1,0:T(8,128)(2,1)S(1)}, u32[]{:S(2)}, u32[]{:S(2)}) collective-permute-start(bf16[256,512]{1,0:T(8,128)(2,1)S(1)} %collective-permute-done.2), channel_id=1, source_target_pairs={{28,0},{0,4},{4,8},{8,12},{12,16},{16,20},{20,24},{24,28},{29,1},{... | collective-permute-start | bytes 786440 | tf_op jit(solution)/shard_map/ppermute | solution.py:10
where the time goes:
time: 76.1 us; the launch traced here: 75.8 us
  waiting for transfers between devices  44.8 us (59%)
  blocking collectives  17.1 us (22%)
  starting transfers between devices  5.18 us (7%)
  matrix products  3.08 us (4%)
  local copies, waits for them, and re-layouts  3.07 us (4%)
  between operations  2.66 us (3%)
    ppermute x6, waiting for transfers between devices, shifted(): return lax.ppermute(block, axis, route)  44.8 us
    all_to_all x1, blocking collectives, shards(): lax.all_to_all(running, 'col', split_axis=1, concat_axis=1, tiled=True)  17.1 us
    ppermute x6, starting transfers between devices, shifted(): return lax.ppermute(block, axis, route)  5.18 us
    dot_general x4, matrix products, shards(): jnp.dot(held_amps, held_ints, preferred_element_type=jnp.float32)  3.08 us
  transfers between devices with their start and end apart: 6, of which 4 were waited for; matrix products, arithmetic and copies ran while one was open for 4% of the time, Pallas kernels for 0%

commit v1 on v0

--- a/solution.py
+++ b/solution.py
@@ -26,7 +26,18 @@
         if offset + 1 < col_count:
             held_amps = shifted(held_amps, "row", 1)
             held_ints = shifted(held_ints, "col", 1)
-    owned = lax.all_to_all(running, "col", split_axis=1, concat_axis=1, tiled=True)
+    frame_out, response = (jax.lax.psum(1, "col"), jax.lax.axis_index("col"))
+    raw_out = list(running.shape)
+    y1 = running.shape[1] // frame_out
+    raw_out[1] = y1
+    reply = raw_out[1]
+    raw_out[1] = reply * frame_out
+    owned = jnp.zeros(raw_out, running.dtype)
+    for pp in tuple(range(frame_out)):
+        aux = lax.dynamic_slice_in_dim(running, (response ^ pp) * y1, y1, axis=1)
+        if pp:
+            aux = jax.lax.ppermute(aux, "col", [(rr, rr ^ pp) for rr in range(frame_out)])
+        owned = lax.dynamic_update_slice_in_dim(owned, aux, (response ^ pp) * reply, axis=1)
     return owned.reshape(1, owned.shape[0], owned.shape[1])
 
 

time: 76.1 us -> 71.8 us (0.943)
  blocking collectives: 17.1 us -> 0 us
  waiting for transfers between devices: 44.8 us -> 56.6 us
  starting transfers between devices: 5.18 us -> 7.11 us
    all_to_all x1 -> x0, blocking collectives: 17.1 us -> none  [shards(): lax.all_to_all(running, 'col', split_axis=1, concat_axis=1, tiled=True)]
    ppermute x0 -> x3, waiting for transfers between devices: none -> 11.8 us  [shards(): jax.lax.ppermute(aux, 'col', [(rr, rr ^ pp) for rr in range(frame_out)])]
    ppermute x0 -> x3, starting transfers between devices: none -> 1.93 us  [shards(): jax.lax.ppermute(aux, 'col', [(rr, rr ^ pp) for rr in range(frame_out)])]
    reshape x1, local copies, waits for them, and re-layouts: 1.31 us -> 0.11 us  [shards(): return owned.reshape(1, owned.shape[0], owned.shape[1])]
    dynamic_update_slice x0 -> x4, local copies, waits for them, and re-layouts: none -> 0.8 us  [shards(): lax.dynamic_update_slice_in_dim(owned, aux, (response ^ pp) * reply, axis=1)]
  transfers between devices with their start and end apart: 6 -> 9, of which waited for: 4 -> 6; matrix products, arithmetic and copies ran while one was open for 4% -> 5% of each run, Pallas kernels for 0% -> 0%
where the time goes in v1:
time: 71.8 us; the launch traced here: 71.7 us
  waiting for transfers between devices  56.6 us (79%)
  starting transfers between devices  7.11 us (10%)
  matrix products  3.08 us (4%)
  between operations  2.59 us (4%)
  local copies, waits for them, and re-layouts  2.32 us (3%)
    ppermute x6, waiting for transfers between devices, shifted(): return lax.ppermute(block, axis, route)  44.8 us
    ppermute x3, waiting for transfers between devices, shards(): jax.lax.ppermute(aux, 'col', [(rr, rr ^ pp) for rr in range(frame_out)])  11.8 us
    ppermute x6, starting transfers between devices, shifted(): return lax.ppermute(block, axis, route)  5.18 us
    dot_general x4, matrix products, shards(): jnp.dot(held_amps, held_ints, preferred_element_type=jnp.float32)  3.08 us
    ppermute x3, starting transfers between devices, shards(): jax.lax.ppermute(aux, 'col', [(rr, rr ^ pp) for rr in range(frame_out)])  1.93 us
  transfers between devices with their start and end apart: 9, of which 6 were waited for; matrix products, arithmetic and copies ran while one was open for 5% of the time, Pallas kernels for 0%

profile of v1, /device:TPU:0, one launch (start us, length us, event | category | flops | bytes accessed | tf_op | source)
XLA Modules:
  0.0 71.7 jit_solution(3235659751015522897)
XLA Ops:
  0.0 0.5 collective-permute-start.1
  0.5 14.6 %collective-permute-done.1 = bf16[512,1024]{1,0:T(8,128)(2,1)S(1)} collective-permute-done((bf16[512,1024]{1,0:T(8,128)(2,1)}, bf16[512,1024]{1,0:T(8,128)(2,1)S(1)}, u32[]{:S(2)}, u32[]{:S(2)}) %collective-permute-start.1) | collective-permute-done | bytes 1048608 | tf_op jit(solution)/shard_map/ppermute | solution.py:10
  15.1 0.0 collective-permute-start.3
  15.1 2.3 %collective-permute-start = (bf16[256,512]{1,0:T(8,128)(2,1)}, bf16[256,512]{1,0:T(8,128)(2,1)S(1)}, u32[]{:S(2)}, u32[]{:S(2)}) collective-permute-start(bf16[256,512]{1,0:T(8,128)(2,1)} %param.3), channel_id=1, source_target_pairs={{28,0},{0,4},{4,8},{8,12},{12,16},{16,20},{20,24},{24,28},{29,1},{... | collective-permute-start | bytes 786440 | tf_op jit(solution)/shard_map/ppermute | solution.py:10
  17.4 11.9 %collective-permute-done.3 = bf16[512,1024]{1,0:T(8,128)(2,1)S(1)} collective-permute-done((bf16[512,1024]{1,0:T(8,128)(2,1)S(1)}, bf16[512,1024]{1,0:T(8,128)(2,1)S(1)}, u32[]{:S(2)}, u32[]{:S(2)}) %collective-permute-start.3) | collective-permute-done | bytes 1048608 | tf_op jit(solution)/shard_map/ppermute | solution.py:10
  29.3 0.0 collective-permute-start.5
  29.3 0.0 copy-start.1
  29.3 0.7 copy-done.1
  30.0 0.6 fusion.3
  33.1 0.0 collective-permute-done
  33.1 2.4 %collective-permute-start.2 = (bf16[256,512]{1,0:T(8,128)(2,1)S(1)}, bf16[256,512]{1,0:T(8,128)(2,1)S(1)}, u32[]{:S(2)}, u32[]{:S(2)}) collective-permute-start(bf16[256,512]{1,0:T(8,128)(2,1)S(1)} %collective-permute-done), channel_id=1, source_target_pairs={{28,0},{0,4},{4,8},{8,12},{12,16},{16,20},{20,24},{24,28},{29,1},{... | collective-permute-start | bytes 786440 | tf_op jit(solution)/shard_map/ppermute | solution.py:10
  35.5 1.8 %convolution_multiply_fusion.3 = f32[256,1024]{1,0:T(8,128)S(1)} fusion(bf16[256,512]{1,0:T(8,128)(2,1)} %param.3, bf16[512,1024]{1,0:T(8,128)(2,1)} %param.4, f32[]{:T(128)} %bitcast), kind=kOutput, calls=%fused_computation.6 | convolution fusion | flops 268697600 | bytes 2359300 | tf_op jit(solution)/shard_map/dot_general | solution.py:23
  37.3 7.5 %collective-permute-done.2 = bf16[256,512]{1,0:T(8,128)(2,1)S(1)} collective-permute-done((bf16[256,512]{1,0:T(8,128)(2,1)S(1)}, bf16[256,512]{1,0:T(8,128)(2,1)S(1)}, u32[]{:S(2)}, u32[]{:S(2)}) %collective-permute-start.2) | collective-permute-done | bytes 262176 | tf_op jit(solution)/shard_map/ppermute | solution.py:10
  44.8 0.0 collective-permute-start.4
  44.8 0.4 fusion.2
  45.3 0.4 fusion.1
  45.7 10.7 %collective-permute-done.4 = bf16[256,512]{1,0:T(8,128)(2,1)S(1)} collective-permute-done((bf16[256,512]{1,0:T(8,128)(2,1)S(1)}, bf16[256,512]{1,0:T(8,128)(2,1)S(1)}, u32[]{:S(2)}, u32[]{:S(2)}) %collective-permute-start.4) | collective-permute-done | bytes 262176 | tf_op jit(solution)/shard_map/ppermute | solution.py:10
  56.4 0.0 collective-permute-done.5
  56.4 0.4 fusion
  56.9 0.1 constant_dynamic-slice_fusion
  57.0 0.1 collective-permute-start.6
  57.0 1.6 %collective-permute-start.7 = (f32[256,256]{1,0:T(8,128)S(1)}, f32[256,256]{1,0:T(8,128)S(1)}, u32[]{:S(2)}, u32[]{:S(2)}) collective-permute-start(f32[256,256]{1,0:T(8,128)S(1)} %get-tuple-element.6), channel_id=1, source_target_pairs={{0,2},{1,3},{2,0},{3,1},{4,6},{5,7},{6,4},{7,5},{8,10},{9,11},{10,... | collective-permute-start | bytes 786440 | tf_op jit(solution)/shard_map/ppermute | solution.py:39
  58.6 0.3 collective-permute-start.8
  58.9 0.1 reshape.23
  59.1 0.0 collective-permute-done.6
  59.1 7.1 %collective-permute-done.7 = f32[256,256]{1,0:T(8,128)S(1)} collective-permute-done((f32[256,256]{1,0:T(8,128)S(1)}, f32[256,256]{1,0:T(8,128)S(1)}, u32[]{:S(2)}, u32[]{:S(2)}) %collective-permute-start.7) | collective-permute-done | bytes 262176 | tf_op jit(solution)/shard_map/ppermute | solution.py:39
  66.3 0.0 copy-start
  66.3 4.7 %collective-permute-done.8 = f32[256,256]{1,0:T(8,128)S(1)} collective-permute-done((f32[256,256]{1,0:T(8,128)S(1)}, f32[256,256]{1,0:T(8,128)S(1)}, u32[]{:S(2)}, u32[]{:S(2)}) %collective-permute-start.8) | collective-permute-done | bytes 262176 | tf_op jit(solution)/shard_map/ppermute | solution.py:39
  70.9 0.0 copy-done
  70.9 0.7 %bitcast_dynamic-update-slice_fusion = f32[1,256,1024]{2,1,0:T(8,128)} fusion(f32[1,256,1024]{2,1,0:T(8,128)} %copy-done, s32[]{:T(128)S(6)} %select_n.65, f32[256,256]{1,0:T(8,128)S(1)} %collective-permute-done.8), kind=kLoop, calls=%fused_computation.7 | loop fusion | bytes 524292 | tf_op jit(solution)/shard_map/dynamic_update_slice | solution.py:40
  (3 shorter events, 0.1 us)
Async XLA Ops:
  0.0 15.1 %collective-permute-start.1 = (bf16[512,1024]{1,0:T(8,128)(2,1)}, bf16[512,1024]{1,0:T(8,128)(2,1)S(1)}, u32[]{:S(2)}, u32[]{:S(2)}) collective-permute-start(bf16[512,1024]{1,0:T(8,128)(2,1)} %param.4), channel_id=1, source_target_pairs={{3,0},{0,1},{1,2},{2,3},{7,4},{4,5},{5,6},{6,7},{11,8},{8,9},{9,10... | collective-permute-start | bytes 3145736 | tf_op jit(solution)/shard_map/ppermute | solution.py:10
  15.1 14.2 %collective-permute-start.3 = (bf16[512,1024]{1,0:T(8,128)(2,1)S(1)}, bf16[512,1024]{1,0:T(8,128)(2,1)S(1)}, u32[]{:S(2)}, u32[]{:S(2)}) collective-permute-start(bf16[512,1024]{1,0:T(8,128)(2,1)S(1)} %collective-permute-done.1), channel_id=1, source_target_pairs={{3,0},{0,1},{1,2},{2,3},{7,4},{4,5},{5,6},{6,7},{11,8},{8,9},{9,10... | collective-permute-start | bytes 3145736 | tf_op jit(solution)/shard_map/ppermute | solution.py:10
  15.1 18.0 %collective-permute-start = (bf16[256,512]{1,0:T(8,128)(2,1)}, bf16[256,512]{1,0:T(8,128)(2,1)S(1)}, u32[]{:S(2)}, u32[]{:S(2)}) collective-permute-start(bf16[256,512]{1,0:T(8,128)(2,1)} %param.3), channel_id=1, source_target_pairs={{28,0},{0,4},{4,8},{8,12},{12,16},{16,20},{20,24},{24,28},{29,1},{... | collective-permute-start | bytes 786440 | tf_op jit(solution)/shard_map/ppermute | solution.py:10
  29.3 27.1 %collective-permute-start.5 = (bf16[512,1024]{1,0:T(8,128)(2,1)S(1)}, bf16[512,1024]{1,0:T(8,128)(2,1)S(1)}, u32[]{:S(2)}, u32[]{:S(2)}) collective-permute-start(bf16[512,1024]{1,0:T(8,128)(2,1)S(1)} %collective-permute-done.3), channel_id=1, source_target_pairs={{3,0},{0,1},{1,2},{2,3},{7,4},{4,5},{5,6},{6,7},{11,8},{8,9},{9,10... | collective-permute-start | bytes 3145736 | tf_op jit(solution)/shard_map/ppermute | solution.py:10
  29.3 0.7 copy-start.1
  33.1 11.7 %collective-permute-start.2 = (bf16[256,512]{1,0:T(8,128)(2,1)S(1)}, bf16[256,512]{1,0:T(8,128)(2,1)S(1)}, u32[]{:S(2)}, u32[]{:S(2)}) collective-permute-start(bf16[256,512]{1,0:T(8,128)(2,1)S(1)} %collective-permute-done), channel_id=1, source_target_pairs={{28,0},{0,4},{4,8},{8,12},{12,16},{16,20},{20,24},{24,28},{29,1},{... | collective-permute-start | bytes 786440 | tf_op jit(solution)/shard_map/ppermute | solution.py:10
  44.8 11.6 %collective-permute-start.4 = (bf16[256,512]{1,0:T(8,128)(2,1)S(1)}, bf16[256,512]{1,0:T(8,128)(2,1)S(1)}, u32[]{:S(2)}, u32[]{:S(2)}) collective-permute-start(bf16[256,512]{1,0:T(8,128)(2,1)S(1)} %collective-permute-done.2), channel_id=1, source_target_pairs={{28,0},{0,4},{4,8},{8,12},{12,16},{16,20},{20,24},{24,28},{29,1},{... | collective-permute-start | bytes 786440 | tf_op jit(solution)/shard_map/ppermute | solution.py:10
  57.0 2.1 %collective-permute-start.6 = (f32[256,256]{1,0:T(8,128)S(1)}, f32[256,256]{1,0:T(8,128)S(1)}, u32[]{:S(2)}, u32[]{:S(2)}) collective-permute-start(f32[256,256]{1,0:T(8,128)S(1)} %get-tuple-element.7), channel_id=1, source_target_pairs={{0,1},{1,0},{2,3},{3,2},{4,5},{5,4},{6,7},{7,6},{8,9},{9,8},{10,11... | collective-permute-start | bytes 786440 | tf_op jit(solution)/shard_map/ppermute | solution.py:39
  57.0 9.2 %collective-permute-start.7 = (f32[256,256]{1,0:T(8,128)S(1)}, f32[256,256]{1,0:T(8,128)S(1)}, u32[]{:S(2)}, u32[]{:S(2)}) collective-permute-start(f32[256,256]{1,0:T(8,128)S(1)} %get-tuple-element.6), channel_id=1, source_target_pairs={{0,2},{1,3},{2,0},{3,1},{4,6},{5,7},{6,4},{7,5},{8,10},{9,11},{10,... | collective-permute-start | bytes 786440 | tf_op jit(solution)/shard_map/ppermute | solution.py:39
  58.6 12.3 %collective-permute-start.8 = (f32[256,256]{1,0:T(8,128)S(1)}, f32[256,256]{1,0:T(8,128)S(1)}, u32[]{:S(2)}, u32[]{:S(2)}) collective-permute-start(f32[256,256]{1,0:T(8,128)S(1)} %get-tuple-element.5), channel_id=1, source_target_pairs={{0,3},{1,2},{2,1},{3,0},{4,7},{5,6},{6,5},{7,4},{8,11},{9,10},{10,... | collective-permute-start | bytes 786440 | tf_op jit(solution)/shard_map/ppermute | solution.py:39
  66.3 4.7 %copy-start = (f32[1,256,1024]{2,1,0:T(8,128)}, f32[1,256,1024]{2,1,0:T(8,128)S(1)}, u32[]{:S(2)}) copy-start(f32[1,256,1024]{2,1,0:T(8,128)S(1)} %bitcast_dynamic-update-slice_fusion.1) | copy-start | bytes 3145732
